TPU v7x, 512 devices: a whole 4x8x8 slice. The times are simulated.
512 devices in a mesh: dp: 64 (over y, x, core), mp: 8 (over z).
Axes of the slice: x: 4, y: 8, z: 8, core: 2. Of those that a mesh axis runs over, the one named last changes fastest.
Arguments:
- tokens: bfloat16 [32768, 2048], P('dp'), may hold values from -6 to 6
- q_weight: bfloat16 [2048, 256], P('dp', 'mp'), may hold values from -0.125 to 0.125
- k_weight: bfloat16 [2048, 256], P('dp', 'mp'), may hold values from -0.125 to 0.125
- v_weight: bfloat16 [2048, 2048], P('dp', 'mp'), may hold values from -0.125 to 0.125
- adapter_down: bfloat16 [2048, 256], P(None, 'mp'), may hold values from -0.125 to 0.125
- adapter_up: bfloat16 [256, 2048], P(None, 'mp'), may hold values from -1.5 to 1.5
- lengths: int32 [4], replicated, may hold values from 1 to 16384, 32768 in all
- adapter_ids: int32 [4], replicated, may hold values from 0 to 15
- head_gain: float32 [2048], P('mp'), may hold values from 0.1 to 1.9
- out_weight: bfloat16 [2048, 2048], P('mp', 'dp'), may hold values from -0.125 to 0.125
Outputs:
- layer_out: bfloat16 [32768, 2048], P('dp', 'mp')
Inputs may be any that keep to these rules, and one draw needn't show every extreme that they name: The lengths sum to 32768 and the longest request has exactly 32768 // 2 tokens.
All inputs are finite; a program needn't handle non-finite values.
Results may differ from a plain program's by a relative error of at most 0.022.
Values may be sent and summed in bfloat16 or wider, within the bound.
A program may use at most 128 MiB of HBM per device.

v0:
```python
import math
import jax
import jax.numpy as jnp
from jax import lax
from jax.sharding import PartitionSpec as P

F = 16
R = 16
EPSILON = 1e-05


def carried_in(value, axis, combine, identity):
    length, place = (lax.axis_size(axis), lax.axis_index(axis))
    everything = jax.tree.map(
        lambda part, kind: lax.all_gather(part.astype(kind), axis),
        value,
        (jnp.bfloat16, jnp.bfloat16),
    )
    start = jax.tree.map(
        lambda part, zero: jnp.broadcast_to(jnp.asarray(zero, part.dtype), part.shape),
        value,
        identity,
    )

    def turn(k, before):
        reached = k < place
        new = combine(
            before, jax.tree.map(lambda part, own: part[k].astype(own.dtype), everything, value)
        )
        return jax.tree.map(lambda a, b: jnp.where(reached, a, b), new, before)

    return lax.fori_loop(0, length, turn, start)


def taylor(inputs):
    squares = (inputs[..., :, None] * inputs[..., None, :]).reshape(
        inputs.shape[:-1] + (inputs.shape[-1] * inputs.shape[-1],)
    )
    constant = jnp.ones(inputs.shape[:-1] + (1,), jnp.float32)
    return jnp.concatenate([constant, 0.5 * inputs, squares * (0.25 / math.sqrt(2.0))], axis=-1)


def token_tables(lengths, adapter_ids, positions):
    bounds = jnp.cumsum(lengths)
    request = jnp.sum((positions[:, None] >= bounds[None, :]).astype(jnp.int32), axis=1)
    openings = bounds - lengths
    starts = jnp.any(positions[:, None] == openings[None, :], axis=1)
    picked = request[:, None] == jnp.arange(lengths.shape[0], dtype=jnp.int32)[None, :]
    adapter = jnp.sum(jnp.where(picked, adapter_ids[None, :], 0), axis=1)
    return (request, starts, adapter)


def block_local(query, key_rows, values, request, starts):
    scores = jnp.einsum("ihd,jhd->hij", query, key_rows, preferred_element_type=jnp.float32) * 0.25
    weights = 1.0 + scores + 0.5 * scores * scores
    indexes = jnp.arange(request.shape[0], dtype=jnp.int32)
    allowed = (indexes[None, :] <= indexes[:, None]) & (request[None, :] == request[:, None])
    weights = jnp.where(allowed[None], weights, 0.0).astype(jnp.bfloat16)
    within = jnp.einsum("hij,jhe->ihe", weights, values, preferred_element_type=jnp.float32)
    query_map = taylor(query.astype(jnp.float32)).astype(jnp.bfloat16)
    key_map = taylor(key_rows.astype(jnp.float32)).astype(jnp.bfloat16)
    tail_mask = (request == request[-1]).astype(jnp.bfloat16)
    masked_keys = key_map * tail_mask[:, None, None]
    summary = jnp.einsum("ihf,ihe->hfe", masked_keys, values, preferred_element_type=jnp.float32)
    restart = jnp.max(starts.astype(jnp.float32))
    return (within, query_map, summary, restart)


def finish(within, query_map, carried, request, starts, gains):
    follows = ((request == request[0]) & jnp.logical_not(starts[0])).astype(jnp.float32)
    cross = jnp.einsum(
        "ihf,hfe->ihe", query_map, carried.astype(jnp.bfloat16), preferred_element_type=jnp.float32
    )
    combined = within + follows[:, None, None] * cross
    factor = lax.rsqrt(jnp.mean(combined * combined, axis=-1, keepdims=True) + EPSILON)
    return (combined * factor * gains[None]).astype(jnp.bfloat16)


def combine(earlier, later):
    return (
        jnp.maximum(earlier[0], later[0]),
        jnp.where(later[0] > 0, later[1], earlier[1] + later[1]),
    )


def per_device(
    tokens,
    q_weight,
    k_weight,
    v_weight,
    adapter_down,
    adapter_up,
    lengths,
    adapter_ids,
    head_gain,
    out_weight,
):
    row_count = tokens.shape[0]
    heads_here = q_weight.shape[1] // F
    value_width = v_weight.shape[1] // heads_here
    positions = lax.axis_index("dp") * row_count + jnp.arange(row_count, dtype=jnp.int32)
    request, starts, adapter = token_tables(lengths, adapter_ids, positions)
    query_sum = jnp.dot(
        tokens,
        lax.all_gather(q_weight, "dp", axis=0, tiled=True),
        preferred_element_type=jnp.float32,
    )
    key_sum = jnp.dot(
        tokens,
        lax.all_gather(k_weight, "dp", axis=0, tiled=True),
        preferred_element_type=jnp.float32,
    )
    value_sum = jnp.dot(
        tokens,
        lax.all_gather(v_weight, "dp", axis=0, tiled=True),
        preferred_element_type=jnp.float32,
    )
    query = query_sum.astype(jnp.bfloat16).reshape(row_count, heads_here, F)
    key_rows = key_sum.astype(jnp.bfloat16).reshape(row_count, heads_here, F)
    piece = lax.all_gather(adapter_down, "mp", axis=1, tiled=True)
    partial_low = jnp.dot(tokens, piece, preferred_element_type=jnp.float32)
    owners = jnp.arange(piece.shape[1], dtype=jnp.int32) // R
    low_rank = jnp.where(adapter[:, None] == owners[None, :], partial_low, 0.0).astype(jnp.bfloat16)
    values = value_sum + jnp.dot(low_rank, adapter_up, preferred_element_type=jnp.float32)
    values = values.astype(jnp.bfloat16).reshape(row_count, heads_here, value_width)
    within, query_map, summary, restart = block_local(query, key_rows, values, request, starts)
    identity = (jnp.zeros((), jnp.float32), jnp.zeros_like(summary))
    _, carried = carried_in((restart, summary), "dp", combine, identity)
    gains = head_gain.reshape(heads_here, value_width)
    normed = finish(within, query_map, carried, request, starts, gains).reshape(
        row_count, heads_here * value_width
    )
    partial_terms = jnp.dot(
        normed,
        lax.all_gather(out_weight, "dp", axis=1, tiled=True),
        preferred_element_type=jnp.float32,
    )
    return lax.psum_scatter(
        partial_terms.astype(jnp.bfloat16), "mp", scatter_dimension=1, tiled=True
    )


def solution(mesh):
    placed = (
        P("dp", None),
        P("dp", "mp"),
        P("dp", "mp"),
        P("dp", "mp"),
        P(None, "mp"),
        P(None, "mp"),
        P(),
        P(),
        P("mp"),
        P("mp", "dp"),
    )
    return jax.shard_map(
        per_device, mesh=mesh, in_specs=placed, out_specs=P("dp", "mp"), check_vma=False
    )
```

profile of v0, /device:TPU:6, one launch (start us, length us, event | category | flops | bytes accessed | tf_op | source)
XLA Modules:
  0.0 530.6 jit_solution(14623870171346762429)
XLA Ops:
  9.7 52.8 %all_gather.30 = bf16[2048,32]{1,0:T(8,128)(2,1)S(1)} all-gather(bf16[32,32]{1,0:T(8,128)(2,1)} %param.14), channel_id=1, replica_groups=mesh['dp'=64,'mp'=8] {'dp'}, dimensions={0}, use_global_device_ids=true | all-gather | bytes 133120 | tf_op jit(solution)/shard_map/all_gather | solution.py:110
  64.0 1.3 compare_convert_fusion
  65.5 2.2 fusion.6
  67.7 70.5 %all-gather.6.cloned.1.call-done = bf16[2048,256]{1,0:T(8,128)(2,1)} async-done(((bf16[32,256]{1,0:T(8,128)(2,1)}), bf16[2048,256]{1,0:T(8,128)(2,1)}) %all-gather.6.cloned.1.call-update) | async-done | bytes 1048592 | tf_op jit(solution)/shard_map/all_gather | solution.py:115
  138.2 2.0 fusion.4
  140.9 1.1 convolution_convert_fusion.1
  143.5 48.5 %all_gather.29 = bf16[2048,32]{1,0:T(8,128)(2,1)S(1)} all-gather(bf16[32,32]{1,0:T(8,128)(2,1)S(1)} %copy-done.1), channel_id=1, replica_groups=mesh['dp'=64,'mp'=8] {'dp'}, dimensions={0}, use_global_device_ids=true | all-gather | bytes 133120 | tf_op jit(solution)/shard_map/all_gather | solution.py:105
  192.8 1.3 dynamic-slice
  194.1 1.4 dynamic-update-slice
  195.6 113.9 %all-reduce = bf16[64]{0:T(256)(128)(2,1)S(1)} all-reduce(bf16[64]{0:T(256)(128)(2,1)S(1)} %dynamic-update-slice), channel_id=1, replica_groups=mesh['dp'=64,'mp'=8] {'dp'}, use_global_device_ids=true, to_apply=%add | all-reduce | flops 64 | bytes 256
  309.5 2.8 fusion.1
  312.3 149.2 %while.14 = (s32[]{:T(128)}, f32[2,273,128]{2,1,0:T(8,128)S(1)}, s32[]{:T(128)}, bf16[64]{0:T(256)(128)(2,1)S(1)}, bf16[64,2,273,128]{3,2,1,0:T(8,128)(2,1)}, /*index=5*/s32[]{:T(128)}, s32[]{:T(128)}, f32[1]{0:T(128)}) while((s32[]{:T(128)}, f32[2,273,128]{2,1,0:T(8,128)S(1)}, s32[]{:T(128)}, bf16[64]{0:T(256)(128)(2,1)S(1)}, ...), condition=%wide.region_6.7_spmd.clone, body=%wide.region_5.6_spmd.clone.sunk | while | flops 349445 | bytes 699005 | solution.py:32
  315.9 1.1 fusion.52
  318.2 1.1 fusion.52
  320.6 1.1 fusion.52
  322.9 1.1 fusion.52
  325.2 1.1 fusion.52
  327.5 1.1 fusion.52
  329.9 1.1 fusion.52
  332.2 1.1 fusion.52
  334.5 1.1 fusion.52
  336.9 1.1 fusion.52
  341.5 1.1 fusion.52
  343.9 1.1 fusion.52
  346.2 1.1 fusion.52
  350.9 1.1 fusion.52
  353.2 1.1 fusion.52
  355.5 1.1 fusion.52
  360.2 1.1 fusion.52
  362.5 1.1 fusion.52
  364.9 1.1 fusion.52
  367.2 1.1 fusion.52
  369.5 1.1 fusion.52
  371.9 1.1 fusion.52
  374.2 1.1 fusion.52
  376.5 1.1 fusion.52
  378.9 1.1 fusion.52
  381.2 1.1 fusion.52
  385.9 1.1 fusion.52
  388.2 1.1 fusion.52
  390.5 1.1 fusion.52
  395.2 1.1 fusion.52
  397.5 1.1 fusion.52
  399.8 1.1 fusion.52
  404.5 1.1 fusion.52
  406.8 1.1 fusion.52
  409.2 1.1 fusion.52
  411.5 1.1 fusion.52
  413.8 1.1 fusion.52
  416.2 1.1 fusion.52
  418.5 1.1 fusion.52
  420.8 1.1 fusion.52
  423.2 1.1 fusion.52
  425.5 1.1 fusion.52
  430.2 1.1 fusion.52
  432.5 1.1 fusion.52
  434.8 1.1 fusion.52
  439.5 1.1 fusion.52
  441.8 1.1 fusion.52
  444.2 1.1 fusion.52
  448.8 1.1 fusion.52
  461.6 1.5 multiply_reduce_fusion
  463.3 3.3 convolution_convert_fusion
  466.6 57.5 %reduce-scatter.2.cloned.1.call-done = bf16[512,256]{1,0:T(8,128)(2,1)} async-done(((bf16[512,2048]{1,0:T(8,128)(2,1)}), bf16[512,256]{1,0:T(8,128)(2,1)}) %reduce-scatter.2.cloned.1.call-update) | async-done | bytes 262160 | tf_op jit(solution)/shard_map/reduce_scatter | solution.py:138
  (127 shorter events, 61.4 us)
Async XLA Ops:
  6.5 56.0 %copy-start = (bf16[512,2048]{1,0:T(8,128)(2,1)S(1)}, bf16[512,2048]{1,0:T(8,128)(2,1)}, u32[]{:S(2)}) copy-start(bf16[512,2048]{1,0:T(8,128)(2,1)} %param.12) | copy-start | bytes 6291460
  6.5 57.4 %copy-start.3 = (s32[4]{0:T(128)S(1)}, s32[4]{0:T(128)}, u32[]{:S(2)}) copy-start(s32[4]{0:T(128)} %param.19) | copy-start | bytes 52
  6.5 58.9 %copy-start.4 = (bf16[256,256]{1,0:T(8,128)(2,1)S(1)}, bf16[256,256]{1,0:T(8,128)(2,1)}, u32[]{:S(2)}) copy-start(bf16[256,256]{1,0:T(8,128)(2,1)} %param.17) | copy-start | bytes 393220
  6.5 58.9 %all-gather.8.cloned.1.call-start = ((), (), s32[]{:S(2)}) async-start(), calls=%async_computation.2 | async-start | bytes 1179648 | tf_op jit(solution)/shard_map/all_gather | solution.py:120
  7.3 130.9 %all-gather.6.cloned.1.call-start = ((), (), s32[]{:S(2)}) async-start(), calls=%async_computation.1 | async-start | bytes 1064960 | tf_op jit(solution)/shard_map/all_gather | solution.py:115
  8.0 304.3 %all-gather.12.cloned.1.call-start = ((), (), s32[]{:S(2)}) async-start(), calls=%async_computation.5 | async-start | bytes 9318400 | tf_op jit(solution)/shard_map/all_gather | solution.py:15
  140.2 0.7 copy-start.5
  140.2 3.3 copy-start.1
  142.0 321.2 %all-gather.10.cloned.1.call-start = ((), (), s32[]{:S(2)}) async-start(), calls=%async_computation.3 | async-start | bytes 1064960 | tf_op jit(solution)/shard_map/all_gather | solution.py:135
  142.6 381.5 %reduce-scatter.2.cloned.1.call-start = ((), (), s32[]{:S(2)}) async-start(), calls=%async_computation.4 | async-start | bytes 2359296 | tf_op jit(solution)/shard_map/reduce_scatter | solution.py:138
  312.3 150.8 %copy-start.2 = (f32[256]{0:T(256)S(1)}, f32[256]{0:T(256)}, u32[]{:S(2)}) copy-start(f32[256]{0:T(256)} %param.20) | copy-start | bytes 3076
Sparse Core Ops, SparseCore 0:
  9.4 46.9 all-gather.7
  59.7 78.4 all-gather.5
  142.1 86.8 all-gather.11
  232.3 80.0 all-gather.9
  466.7 57.2 reduce-scatter.1
where the time goes:
time: 533 us; the launch traced here: 531 us
  blocking collectives  215 us (40%)
  waiting for transfers between devices  130 us (24%)
  other arithmetic  72.4 us (14%)
  loops' own time  43.5 us (8%)
  local copies, waits for them, and re-layouts  41.7 us (8%)
  matrix products  14.4 us (3%)
  between operations  13.4 us (3%)
    unnamed x1, blocking collectives  114 us
    all_gather x1, waiting for transfers between devices, per_device(): lax.all_gather(v_weight, 'dp', axis=0, tiled=True)  70.5 us
    select_n x64, other arithmetic, turn(): return jax.tree.map(lambda a, b: jnp.where(reached, a, b), new, before)  68.1 us
    reduce_scatter x1, waiting for transfers between devices, per_device(): lax.psum_scatter(partial_terms.astype(jnp.bfloat16), 'mp', scatter_dimens...  57.5 us
    all_gather x1, blocking collectives, per_device(): lax.all_gather(k_weight, 'dp', axis=0, tiled=True)  52.8 us
    all_gather x1, blocking collectives, per_device(): lax.all_gather(q_weight, 'dp', axis=0, tiled=True)  48.5 us
    another operation x1, loops' own time, carried_in(): return lax.fori_loop(0, length, turn, start)  43.5 us
    dynamic_slice x64, local copies, waits for them, and re-layouts, turn(): part[k].astype(own.dtype)  37.6 us
  transfers between devices with their start and end apart: 5, of which 2 were waited for; matrix products, arithmetic and copies ran while one was open for 23% of the time, Pallas kernels for 0%

commit v1 on v0

--- a/solution.py
+++ b/solution.py
@@ -7,6 +7,13 @@
 F = 16
 R = 16
 EPSILON = 1e-05
+
+
+def all_by_exchange(array, mesh_axis, dim):
+    size = lax.axis_size(mesh_axis)
+    pieces = jnp.stack([array for _ in range(size)])
+    pieces = lax.all_to_all(pieces, mesh_axis, split_axis=0, concat_axis=0)
+    return jnp.concatenate(pieces, axis=dim)
 
 
 def carried_in(value, axis, combine, identity):
@@ -111,9 +118,7 @@
         preferred_element_type=jnp.float32,
     )
     value_sum = jnp.dot(
-        tokens,
-        lax.all_gather(v_weight, "dp", axis=0, tiled=True),
-        preferred_element_type=jnp.float32,
+        tokens, all_by_exchange(v_weight, "dp", 0), preferred_element_type=jnp.float32
     )
     query = query_sum.astype(jnp.bfloat16).reshape(row_count, heads_here, F)
     key_rows = key_sum.astype(jnp.bfloat16).reshape(row_count, heads_here, F)

time: 533 us -> 492 us (0.923)
  waiting for transfers between devices: 130 us -> 63.1 us
  blocking collectives: 215 us -> 230 us
  starting transfers between devices: 0.16 us -> 10.7 us
    all_gather x1 -> x0, waiting for transfers between devices: 70.5 us -> none  [per_device(): lax.all_gather(v_weight, 'dp', axis=0, tiled=True)]
    all_gather x1, blocking collectives: 52.8 us -> 67.7 us  [per_device(): lax.all_gather(k_weight, 'dp', axis=0, tiled=True)]
    all_to_all x0 -> x1, starting transfers between devices: none -> 10.6 us  [all_by_exchange(): pieces = lax.all_to_all(pieces, mesh_axis, split_axis=0, concat_axis=0)]
  transfers between devices with their start and end apart: 5 -> 5, of which waited for: 2 -> 1; matrix products, arithmetic and copies ran while one was open for 23% -> 25% of each run, Pallas kernels for 0% -> 0%
where the time goes in v1:
time: 492 us; the launch traced here: 490 us
  blocking collectives  230 us (47%)
  other arithmetic  71.9 us (15%)
  waiting for transfers between devices  63.1 us (13%)
  loops' own time  43.5 us (9%)
  local copies, waits for them, and re-layouts  43.3 us (9%)
  matrix products  14 us (3%)
  between operations  13.4 us (3%)
  starting transfers between devices  10.7 us (2%)
    unnamed x1, blocking collectives  115 us
    select_n x64, other arithmetic, turn(): return jax.tree.map(lambda a, b: jnp.where(reached, a, b), new, before)  68.1 us
    all_gather x1, blocking collectives, per_device(): lax.all_gather(k_weight, 'dp', axis=0, tiled=True)  67.7 us
    reduce_scatter x1, waiting for transfers between devices, per_device(): lax.psum_scatter(partial_terms.astype(jnp.bfloat16), 'mp', scatter_dimens...  61.7 us
    all_gather x1, blocking collectives, per_device(): lax.all_gather(q_weight, 'dp', axis=0, tiled=True)  47.8 us
    another operation x1, loops' own time, carried_in(): return lax.fori_loop(0, length, turn, start)  43.5 us
    dynamic_slice x64, local copies, waits for them, and re-layouts, turn(): part[k].astype(own.dtype)  37.6 us
    all_to_all x1, starting transfers between devices, all_by_exchange(): pieces = lax.all_to_all(pieces, mesh_axis, split_axis=0, concat_axis=0)  10.6 us
  transfers between devices with their start and end apart: 5, of which 1 were waited for; matrix products, arithmetic and copies ran while one was open for 25% of the time, Pallas kernels for 0%

profile of v1, /device:TPU:6, one launch (start us, length us, event | category | flops | bytes accessed | tf_op | source)
XLA Modules:
  0.0 490.1 jit_solution(12692136405493997413)
XLA Ops:
  7.3 1.9 stack.2
  9.1 10.6 %all-to-all-start = ((bf16[64,32,256]{2,1,0:T(8,128)(2,1)}), bf16[64,32,256]{2,1,0:T(8,128)(2,1)S(1)}, u32[]{:S(2)}, u32[]{:S(2)}) async-start(bf16[64,32,256]{2,1,0:T(8,128)(2,1)} %stack.2), calls=%async_computation | async-start | bytes 2097152 | tf_op jit(solution)/shard_map/all_to_all | solution.py:15
  20.1 67.7 %all_gather.26 = bf16[2048,32]{1,0:T(8,128)(2,1)S(1)} all-gather(bf16[32,32]{1,0:T(8,128)(2,1)S(1)} %copy-done.2), channel_id=1, replica_groups=mesh['dp'=64,'mp'=8] {'dp'}, dimensions={0}, use_global_device_ids=true | all-gather | bytes 133120 | tf_op jit(solution)/shard_map/all_gather | solution.py:117
  89.4 1.3 compare_convert_fusion
  91.6 3.0 fusion.6
  94.6 1.9 fusion.4
  97.2 1.1 convolution_convert_fusion.1
  100.0 47.8 %all_gather.25 = bf16[2048,32]{1,0:T(8,128)(2,1)S(1)} all-gather(bf16[32,32]{1,0:T(8,128)(2,1)S(1)} %copy-done.3), channel_id=1, replica_groups=mesh['dp'=64,'mp'=8] {'dp'}, dimensions={0}, use_global_device_ids=true | all-gather | bytes 133120 | tf_op jit(solution)/shard_map/all_gather | solution.py:112
  148.6 1.2 dynamic-slice
  149.8 1.3 dynamic-update-slice
  151.1 114.6 %all-reduce = bf16[64]{0:T(256)(128)(2,1)S(1)} all-reduce(bf16[64]{0:T(256)(128)(2,1)S(1)} %dynamic-update-slice), channel_id=1, replica_groups=mesh['dp'=64,'mp'=8] {'dp'}, use_global_device_ids=true, to_apply=%add | all-reduce | flops 64 | bytes 256
  265.8 2.8 fusion.1
  268.6 149.2 %while.14 = (s32[]{:T(128)}, f32[2,273,128]{2,1,0:T(8,128)S(1)}, s32[]{:T(128)}, bf16[64]{0:T(256)(128)(2,1)S(1)}, bf16[64,2,273,128]{3,2,1,0:T(8,128)(2,1)}, /*index=5*/s32[]{:T(128)}, s32[]{:T(128)}, f32[1]{0:T(128)}) while((s32[]{:T(128)}, f32[2,273,128]{2,1,0:T(8,128)S(1)}, s32[]{:T(128)}, bf16[64]{0:T(256)(128)(2,1)S(1)}, ...), condition=%wide.region_6.7_spmd.clone, body=%wide.region_5.6_spmd.clone.sunk | while | flops 349445 | bytes 699005 | solution.py:39
  272.2 1.1 fusion.52
  274.5 1.1 fusion.52
  276.8 1.1 fusion.52
  279.2 1.1 fusion.52
  281.5 1.1 fusion.52
  283.8 1.1 fusion.52
  286.2 1.1 fusion.52
  288.5 1.1 fusion.52
  290.8 1.1 fusion.52
  293.2 1.1 fusion.52
  297.8 1.1 fusion.52
  300.2 1.1 fusion.52
  302.5 1.1 fusion.52
  307.2 1.1 fusion.52
  309.5 1.1 fusion.52
  311.8 1.1 fusion.52
  316.5 1.1 fusion.52
  318.8 1.1 fusion.52
  321.1 1.1 fusion.52
  323.5 1.1 fusion.52
  325.8 1.1 fusion.52
  328.1 1.1 fusion.52
  330.5 1.1 fusion.52
  332.8 1.1 fusion.52
  335.1 1.1 fusion.52
  337.5 1.1 fusion.52
  342.1 1.1 fusion.52
  344.5 1.1 fusion.52
  346.8 1.1 fusion.52
  351.5 1.1 fusion.52
  353.8 1.1 fusion.52
  356.1 1.1 fusion.52
  360.8 1.1 fusion.52
  363.1 1.1 fusion.52
  365.5 1.1 fusion.52
  367.8 1.1 fusion.52
  370.1 1.1 fusion.52
  372.5 1.1 fusion.52
  374.8 1.1 fusion.52
  377.1 1.1 fusion.52
  379.5 1.1 fusion.52
  381.8 1.1 fusion.52
  386.4 1.1 fusion.52
  388.8 1.1 fusion.52
  391.1 1.1 fusion.52
  395.8 1.1 fusion.52
  398.1 1.1 fusion.52
  400.4 1.1 fusion.52
  405.1 1.1 fusion.52
  418.5 3.3 convolution_convert_fusion
  421.9 61.7 %reduce-scatter.2.cloned.1.call-done = bf16[512,256]{1,0:T(8,128)(2,1)} async-done(((bf16[512,2048]{1,0:T(8,128)(2,1)}), bf16[512,256]{1,0:T(8,128)(2,1)}) %reduce-scatter.2.cloned.1.call-update) | async-done | bytes 262160 | tf_op jit(solution)/shard_map/reduce_scatter | solution.py:143
  (135 shorter events, 60.8 us)
Async XLA Ops:
  6.5 81.3 %copy-start = (bf16[512,2048]{1,0:T(8,128)(2,1)S(1)}, bf16[512,2048]{1,0:T(8,128)(2,1)}, u32[]{:S(2)}) copy-start(bf16[512,2048]{1,0:T(8,128)(2,1)} %param.12) | copy-start | bytes 6291460
  6.5 13.3 %copy-start.7 = (s32[4]{0:T(128)S(1)}, s32[4]{0:T(128)}, u32[]{:S(2)}) copy-start(s32[4]{0:T(128)} %param.18) | copy-start | bytes 52
  6.5 13.6 %copy-start.2 = (bf16[32,32]{1,0:T(8,128)(2,1)S(1)}, bf16[32,32]{1,0:T(8,128)(2,1)}, u32[]{:S(2)}) copy-start(bf16[32,32]{1,0:T(8,128)(2,1)} %param.14) | copy-start | bytes 6148
  6.5 85.1 %all-gather.5.cloned.1.call-start = ((), (), s32[]{:S(2)}) async-start(), calls=%async_computation.2 | async-start | bytes 1179648 | tf_op jit(solution)/shard_map/all_gather | solution.py:125
  9.1 85.5 %all-to-all-start = ((bf16[64,32,256]{2,1,0:T(8,128)(2,1)}), bf16[64,32,256]{2,1,0:T(8,128)(2,1)S(1)}, u32[]{:S(2)}, u32[]{:S(2)}) async-start(bf16[64,32,256]{2,1,0:T(8,128)(2,1)} %stack.2), calls=%async_computation | async-start | bytes 2097152 | tf_op jit(solution)/shard_map/all_to_all | solution.py:15
  19.7 69.6 %copy-start.5 = (s32[4]{0:T(128)S(1)}, s32[4]{0:T(128)}, u32[]{:S(2)}) copy-start(s32[4]{0:T(128)} %param.19) | copy-start | bytes 52
  19.7 71.9 %copy-start.6 = (bf16[256,256]{1,0:T(8,128)(2,1)S(1)}, bf16[256,256]{1,0:T(8,128)(2,1)}, u32[]{:S(2)}) copy-start(bf16[256,256]{1,0:T(8,128)(2,1)} %param.17) | copy-start | bytes 393220
  19.7 248.8 %all-gather.9.cloned.1.call-start = ((), (), s32[]{:S(2)}) async-start(), calls=%async_computation.5 | async-start | bytes 9318400 | tf_op jit(solution)/shard_map/all_gather | solution.py:22
  94.6 2.6 copy-start.1
  96.5 0.7 copy-start.8
  96.5 3.5 copy-start.3
  98.4 320.1 %all-gather.7.cloned.1.call-start = ((), (), s32[]{:S(2)}) async-start(), calls=%async_computation.3 | async-start | bytes 1064960 | tf_op jit(solution)/shard_map/all_gather | solution.py:140
  99.1 384.4 %reduce-scatter.2.cloned.1.call-start = ((), (), s32[]{:S(2)}) async-start(), calls=%async_computation.4 | async-start | bytes 2359296 | tf_op jit(solution)/shard_map/reduce_scatter | solution.py:143
  268.6 149.3 %copy-start.9 = (f32[2,128,512]{2,1,0:T(8,128)S(1)}, f32[2,128,512]{2,1,0:T(8,128)}, u32[]{:S(2)}) copy-start(f32[2,128,512]{2,1,0:T(8,128)} %fusion.1) | copy-start | bytes 1572868
  268.6 149.8 %copy-start.4 = (f32[256]{0:T(256)S(1)}, f32[256]{0:T(256)}, u32[]{:S(2)}) copy-start(f32[256]{0:T(256)} %param.20) | copy-start | bytes 3076
Sparse Core Ops, SparseCore 0:
  9.4 46.7 all-gather.4
  98.5 91.2 all-gather.8
  193.1 79.8 all-gather.6
  422.0 61.5 reduce-scatter.1
